TPU v7x, 32 devices: a whole 2x2x4 slice. The times are simulated.
32 devices in a mesh: dp: 8 (over y, x, core), mp: 4 (over z).
Axes of the slice: x: 2, y: 2, z: 4, core: 2. Of those that a mesh axis runs over, the one named last changes fastest.
Arguments:
- tokens: bfloat16 [8192, 5120], P('dp'), may hold values from -6 to 6
- norm_gain: bfloat16 [5120], replicated, may hold values from 0.099609375 to 1.8984375
- w_query: bfloat16 [5120, 5120], P('dp', 'mp'), may hold values from -0.078125 to 0.078125
- b_query: bfloat16 [5120], P('mp'), may hold values from -3 to 3
- keyvalue_weight: bfloat16 [5120, 2, 1024], P('dp', None, 'mp'), may hold values from -0.078125 to 0.078125
- b_keyval: bfloat16 [2, 1024], P(None, 'mp'), may hold values from -3 to 3
- w_out: bfloat16 [5120, 5120], P('mp', 'dp'), may hold values from -0.5 to 0.5
- kv_pool: bfloat16 [2, 512, 64, 1024], P(None, 'dp', None, 'mp'), may hold values from -64 to 64
- page_owner: int32 [8, 16], replicated, may hold values from 0 to 7, as said below
- page_index: int32 [8, 16], replicated, may hold values from 0 to 63
- prefix_pages: int32 [8], replicated, may hold values from 10 to 16, as said below
- prompt_device: int32 [8], replicated, may hold values from 0 to 7, each once
Outputs:
- attn_out: bfloat16 [8192, 5120], P('dp', 'mp')
Inputs may be any that keep to these rules, and one draw needn't show every extreme that they name: `page_owner`: slots at or beyond a prompt's prefix_pages are unused. Of one prompt's used slots at most 2 name the same owner, and some prompt has exactly 2 used slots with one owner. `prefix_pages`: some prompt has 16 used slots.
All inputs are finite; a program needn't handle non-finite values.
Results may differ from a plain program's by a relative error of at most 0.014.
The roundings to bfloat16 on the way count: a program that leaves them out, or rounds other values in their place, can miss the bound.
Values may be sent and summed in bfloat16 or wider, within the bound.
A program may use at most 192 MiB of HBM per device.

v0:
```python
import jax
import jax.numpy as jnp
from jax import lax
from jax.sharding import PartitionSpec as P

HD = 128
CAP = 2
rope_theta = 1000000.0
norm_eps = 1e-06
masked_score = -1e30


def rms_normed(rows, norm_gain):
    values = rows.astype(jnp.float32)
    inverse = lax.rsqrt(jnp.mean(values * values, axis=-1, keepdims=True) + norm_eps)
    return (values * inverse * norm_gain.astype(jnp.float32)).astype(jnp.bfloat16)


def rotary(values, positions):
    half_dim = values.shape[-1] // 2
    frequency = rope_theta ** (-jnp.arange(half_dim, dtype=jnp.float32) * 2.0 / values.shape[-1])
    angles = positions.astype(jnp.float32)[:, None] * frequency[None, :]
    cosine = jnp.cos(angles)[:, None, :]
    sine_part = jnp.sin(angles)[:, None, :]
    front_half = values[..., :half_dim]
    back_half = values[..., half_dim:]
    return jnp.concatenate(
        [front_half * cosine - back_half * sine_part, back_half * cosine + front_half * sine_part],
        axis=-1,
    )


def shards(
    tokens,
    norm_gain,
    w_query,
    b_query,
    keyvalue_weight,
    b_keyval,
    w_out,
    kv_pool,
    page_owner,
    page_index,
    prefix_pages,
    prompt_device,
):
    groups = lax.axis_size("dp")
    my_group = lax.axis_index("dp")
    seq_rows = tokens.shape[0]
    width_kv = keyvalue_weight.shape[2]
    kv_local = width_kv // HD
    heads_local = w_query.shape[1] // HD
    per_group = heads_local // kv_local
    page_len = kv_pool.shape[2]
    max_pages = page_owner.shape[1]
    group_ids = jnp.arange(groups, dtype=jnp.int32)
    slot_prompt = jnp.sum(
        jnp.where(prompt_device[None, :] == group_ids[:, None], group_ids[None, :], 0), axis=1
    )
    owners_all = jnp.take(page_owner, slot_prompt, axis=0)
    index_all = jnp.take(page_index, slot_prompt, axis=0)
    length_all = jnp.take(prefix_pages, slot_prompt, axis=0)
    slot_ids = jnp.arange(max_pages, dtype=jnp.int32)
    places = jnp.arange(CAP, dtype=jnp.int32)
    used = slot_ids[None, :] < length_all[:, None]
    mine = used & (owners_all == my_group)
    rank = jnp.cumsum(mine.astype(jnp.int32), axis=1) - 1
    chosen = mine[:, None, :] & (rank[:, None, :] == places[None, :, None])
    send_index = jnp.sum(jnp.where(chosen, index_all[:, None, :], 0), axis=2)
    send_live = jnp.any(chosen, axis=2)
    outgoing = jnp.take(kv_pool, send_index.reshape(-1), axis=1).reshape(
        2, groups, CAP, page_len, width_kv
    )
    outgoing = jnp.where(send_live[None, :, :, None, None], outgoing, jnp.zeros((), outgoing.dtype))
    arrived = lax.all_to_all(outgoing, "dp", split_axis=1, concat_axis=1, tiled=True)
    my_owners = jnp.take(owners_all, my_group, axis=0)
    my_length = jnp.take(length_all, my_group, axis=0)
    my_used = slot_ids < my_length
    cached = arrived
    counts = jnp.sum(
        ((my_owners[None, :] == group_ids[:, None]) & my_used[None, :]).astype(jnp.int32), axis=1
    )
    page_live = (places[None, :] < counts[:, None]).reshape(-1)
    cached_count = page_live.shape[0]
    cached = cached.reshape(2, cached_count * page_len, kv_local, HD)
    key_live = jnp.repeat(page_live, page_len)
    normed = rms_normed(tokens, norm_gain)
    columns = normed
    query = jnp.dot(
        columns,
        lax.all_gather(w_query, "dp", axis=0, tiled=True),
        preferred_element_type=jnp.float32,
    )
    piece = lax.all_gather(keyvalue_weight, "dp", axis=0, tiled=True)
    columns = normed
    keyval = jnp.dot(
        columns, piece.reshape(piece.shape[0], 2 * width_kv), preferred_element_type=jnp.float32
    )
    query = query + b_query.astype(jnp.float32)
    keyval = keyval + b_keyval.reshape(2 * width_kv).astype(jnp.float32)
    row_ids = jnp.arange(seq_rows, dtype=jnp.int32)
    positions = my_length * page_len + row_ids
    rotated = rotary(query.reshape(seq_rows, heads_local, HD), positions).astype(jnp.bfloat16)
    new_keys = rotary(keyval[:, :width_kv].reshape(seq_rows, kv_local, HD), positions).astype(
        jnp.bfloat16
    )
    new_values = keyval[:, width_kv:].reshape(seq_rows, kv_local, HD).astype(jnp.bfloat16)
    gathered_keys = jnp.concatenate([cached[0], new_keys], axis=0)
    all_values = jnp.concatenate([cached[1], new_values], axis=0)
    scale = HD ** (-0.5)
    block = min(512, seq_rows)
    outputs = []
    for begin in range(0, seq_rows, block):
        query_block = rotated[begin : begin + block].reshape(block, kv_local, per_group, HD)
        logit_scores = (
            jnp.einsum(
                "qkgd,nkd->kgqn", query_block, gathered_keys, preferred_element_type=jnp.float32
            )
            * scale
        )
        causal = row_ids[None, :] <= (begin + jnp.arange(block, dtype=jnp.int32))[:, None]
        allowed = jnp.concatenate(
            [jnp.broadcast_to(key_live[None, :], (block, key_live.shape[0])), causal], axis=1
        )
        logit_scores = jnp.where(allowed[None, None], logit_scores, masked_score)
        top = jnp.max(logit_scores, axis=-1, keepdims=True)
        raised = jnp.exp(logit_scores - top)
        weights = (raised / jnp.sum(raised, axis=-1, keepdims=True)).astype(jnp.bfloat16)
        attended = jnp.einsum(
            "kgqn,nkd->qkgd", weights, all_values, preferred_element_type=jnp.float32
        ).astype(jnp.bfloat16)
        outputs.append(attended.reshape(block, heads_local * HD))
    attention = jnp.concatenate(outputs, axis=0)
    partial_out = jnp.dot(
        attention,
        lax.all_gather(w_out, "dp", axis=1, tiled=True),
        preferred_element_type=jnp.float32,
    )
    return lax.psum_scatter(partial_out.astype(jnp.bfloat16), "mp", scatter_dimension=1, tiled=True)


def solution(mesh):
    return jax.shard_map(
        shards,
        mesh=mesh,
        in_specs=(
            P("dp", None),
            P(),
            P("dp", "mp"),
            P("mp"),
            P("dp", None, "mp"),
            P(None, "mp"),
            P("mp", "dp"),
            P(None, "dp", None, "mp"),
            P(),
            P(),
            P(),
            P(),
        ),
        out_specs=P("dp", "mp"),
        check_vma=False,
    )
```

profile of v0, /device:TPU:0, one launch (start us, length us, event | category | flops | bytes accessed | tf_op | source)
XLA Modules:
  0.0 446.5 jit_solution(14333312355319830557)
XLA Ops:
  6.5 0.7 all-gather.4.cloned.1.call-update
  7.3 0.7 all-gather.6.cloned.1.call-update
  8.0 0.8 select_reduce_fusion.1
  8.8 1.3 gather_fusion
  10.1 0.6 gather_fusion.2
  10.7 1.2 gather_fusion.3
  12.0 0.2 reduce_window_sum.11
  12.3 0.1 select_reduce_fusion
  12.6 2.8 gather_fusion.1
  15.4 0.1 copy.87
  15.7 0.2 fusion.32
  15.8 0.1 copy.84
  15.9 0.2 select_select_fusion
  16.1 1.1 copy.88
  17.2 5.2 %all-to-all-start = ((bf16[2,8,2,64,256]{4,3,2,0,1:T(8,128)(2,1)}), bf16[2,8,2,64,256]{4,3,2,0,1:T(8,128)(2,1)S(1)}, u32[]{:S(2)}, u32[]{:S(2)}) async-start(bf16[2,8,2,64,256]{4,3,2,0,1:T(8,128)(2,1)} %copy.88), calls=%async_computation | async-start | bytes 2097152 | tf_op jit(solution)/shard_map/all_to_all | solution.py:75
  22.5 0.7 all-gather.8.cloned.1.call-update
  23.2 0.6 dynamic-slice.6
  24.5 0.1 convert_reduce_fusion
  25.0 1.0 multiply_cosine_fusion
  26.0 1.0 copy.91
  27.0 1.0 copy.93
  28.0 6.1 %fusion.4 = f32[1024]{0:T(1024)S(1)} fusion(bf16[1024,5120]{1,0:T(8,128)(2,1)} %param.14), kind=kLoop, calls=%fused_computation.16 | loop fusion | flops 15727616 | bytes 10489856 | tf_op jit(solution)/shard_map/reduce_sum | solution.py:15
  34.1 0.5 iota_compare_fusion
  34.6 2.7 pad_add_fusion
  37.3 4.1 all-to-all-done
  41.5 0.1 squeeze.7
  41.6 0.9 copy.94
  42.5 0.1 squeeze.6
  42.6 1.1 copy.89
  43.7 18.7 %all-gather.4.cloned.1.call-done = bf16[5120,2,256]{2,1,0:T(2,128)(2,1)} async-done(((bf16[640,2,256]{2,1,0:T(2,128)(2,1)}), bf16[5120,2,256]{2,1,0:T(2,128)(2,1)}) %all-gather.4.cloned.1.call-update) | async-done | bytes 5242896 | tf_op jit(solution)/shard_map/all_gather | solution.py:94
  62.4 3.4 copy.106
  65.8 8.9 %fusion.27 = f32[1024,512]{0,1:T(8,128)S(1)} fusion(bf16[5120,512]{1,0:T(8,128)(2,1)S(1)} %bitcast.94, bf16[1024,5120]{1,0:T(8,128)(2,1)} %param.14, f32[5120]{0:T(1024)S(1)} %convert_element_type.65, f32[1024]{0:T(1024)S(1)} %add_rsqrt_fusion, f32[512]{0:T(512)S(1)} %bitcast.102), kind=kOutput, calls=%fused_computation.45 | convolution fusion | flops 5390204928 | bytes 17852416 | tf_op jit(solution)/shard_map/dot_general | solution.py:96
  74.8 0.9 slice.84
  75.8 0.3 copy.104
  76.1 0.3 copy.105
  76.4 2.5 subtract_convert_fusion.1
  79.0 59.6 %all-gather.6.cloned.1.call-done = bf16[5120,1280]{1,0:T(8,128)(2,1)} async-done(((bf16[640,1280]{1,0:T(8,128)(2,1)}), bf16[5120,1280]{1,0:T(8,128)(2,1)}) %all-gather.6.cloned.1.call-update) | async-done | bytes 13107216 | tf_op jit(solution)/shard_map/all_gather | solution.py:91
  138.5 20.0 %convolution_add_fusion = f32[1024,1280]{1,0:T(8,128)} fusion(bf16[5120,1280]{1,0:T(8,128)(2,1)} %all-gather.6.cloned.1.call-done, bf16[1024,5120]{1,0:T(8,128)(2,1)} %param.14, f32[5120]{0:T(1024)S(1)} %convert_element_type.65, f32[1024]{0:T(1024)S(1)} %add_rsqrt_fusion, f32[1280]{0:T(1024)S(1)} %convert_element_type.72), kind=kOutput, calls=%fused_computation.28 | convolution fusion | flops 13444055040 | bytes 28865536 | tf_op jit(solution)/shard_map/dot_general | solution.py:89
  158.5 5.9 %copy.95 = f32[1024,1280]{0,1:T(8,128)} copy(f32[1024,1280]{1,0:T(8,128)} %convolution_add_fusion) | data formatting | bytes 10485760 | tf_op jit(solution)/shard_map/add | solution.py:99
  164.4 3.4 subtract_convert_fusion
  167.8 0.3 fusion.30
  168.1 0.8 copy-done.3
  168.9 22.1 %fusion.50 = (f32[2,5,512]{2,1,0:T(8,128)S(1)}, f32[2,5,512,2048]{2,3,1,0:T(8,128)}) fusion(pred[512,2048]{0,1:T(8,128)(4,1)} %get-tuple-element.45, bf16[512,2,5,128]{0,3,2,1:T(8,128)(2,1)S(1)} %bitcast.99, bf16[1024,2,64]{2,0,1:T(8,128)(2,1)} %get-tuple-element.36, bf16[1024,2,64]{2,0,1:T(8,128)(2,1)} %get-tuple-element.35, ...), kind=kOutput, calls=%fused_computation.102 | convolution fusion | flops 2729445376 | bytes 45371392 | tf_op jit(solution)/shard_map/sub | solution.py:127
  190.9 20.5 %fusion.49 = (f32[2,5,512]{2,1,0:T(8,128)S(1)}, f32[2,5,512,2048]{2,3,1,0:T(8,128)}) fusion(pred[512,2048]{0,1:T(8,128)(4,1)} %get-tuple-element.46, bf16[512,2,5,128]{0,3,2,1:T(8,128)(2,1)S(1)} %bitcast.98, bf16[1024,2,64]{2,0,1:T(8,128)(2,1)} %get-tuple-element.36, bf16[1024,2,64]{2,0,1:T(8,128)(2,1)} %get-tuple-element.35, ...), kind=kOutput, calls=%fused_computation.101 | convolution fusion | flops 2729445376 | bytes 45371392 | tf_op jit(solution)/shard_map/sub | solution.py:127
  211.4 14.7 %fusion.26 = bf16[2,128,5,512]{3,1,2,0:T(8,128)(2,1)S(1)} fusion(f32[2,5,512,2048]{2,3,1,0:T(8,128)} %get-tuple-element.51, f32[2,5,512]{2,1,0:T(8,128)S(1)} %get-tuple-element.50, bf16[1024,2,128]{0,2,1:T(8,128)(2,1)S(1)} %bitcast.100, bf16[1024,2,128]{0,2,1:T(8,128)(2,1)S(1)} %copy-done.2), kind=kOutput, calls=%fused_computation.44 | convolution fusion | flops 2708078592 | bytes 44322816 | tf_op jit(solution)/shard_map/kgqn,nkd->qkgd/dot_general | solution.py:129
  226.1 15.6 %fusion.25 = bf16[2,128,5,512]{3,1,2,0:T(8,128)(2,1)} fusion(f32[2,5,512,2048]{2,3,1,0:T(8,128)} %get-tuple-element.49, f32[2,5,512]{2,1,0:T(8,128)S(1)} %get-tuple-element.48, bf16[1024,2,128]{0,2,1:T(8,128)(2,1)S(1)} %bitcast.101, bf16[1024,2,128]{0,2,1:T(8,128)(2,1)S(1)} %copy-done.2), kind=kOutput, calls=%fused_computation.43 | convolution fusion | flops 2708078592 | bytes 44322816 | tf_op jit(solution)/shard_map/kgqn,nkd->qkgd/dot_general | solution.py:129
  241.7 19.7 %convolution_convert_fusion = bf16[1024,5120]{1,0:T(8,128)(2,1)} fusion(bf16[1280,5120]{1,0:T(8,128)(2,1)} %all-gather.8.cloned.1.call-done, bf16[512,1280]{0,1:T(8,128)(2,1)} %bitcast.104, bf16[512,1280]{0,1:T(8,128)(2,1)S(1)} %bitcast.103), kind=kOutput, calls=%fused_computation.27 | convolution fusion | flops 13432258560 | bytes 26214400 | tf_op jit(solution)/shard_map/dot_general | solution.py:134
  261.5 178.5 %reduce-scatter.2.cloned.1.call-done = bf16[1024,1280]{1,0:T(8,128)(2,1)} async-done(((bf16[1024,5120]{1,0:T(8,128)(2,1)}), bf16[1024,1280]{1,0:T(8,128)(2,1)}) %reduce-scatter.2.cloned.1.call-update) | async-done | bytes 2621456 | tf_op jit(solution)/shard_map/reduce_scatter | solution.py:139
  (51 shorter events, 1.3 us)
Async XLA Ops:
  6.5 3.6 copy-start
  6.5 55.9 %all-gather.4.cloned.1.call-start = ((), (), s32[]{:S(2)}) async-start(), calls=%async_computation.2 | async-start | bytes 5898240 | tf_op jit(solution)/shard_map/all_gather | solution.py:94
  7.3 131.3 %all-gather.6.cloned.1.call-start = ((), (), s32[]{:S(2)}) async-start(), calls=%async_computation.3 | async-start | bytes 14745600 | tf_op jit(solution)/shard_map/all_gather | solution.py:91
  15.5 9.0 %copy-start.5 = (bf16[5120]{0:T(1024)(128)(2,1)S(1)}, bf16[5120]{0:T(1024)(128)(2,1)}, u32[]{:S(2)}) copy-start(bf16[5120]{0:T(1024)(128)(2,1)} %param.15) | copy-start | bytes 30724
  15.5 9.0 %copy-start.6 = (bf16[1280]{0:T(1024)(128)(2,1)S(1)}, bf16[1280]{0:T(1024)(128)(2,1)}, u32[]{:S(2)}) copy-start(bf16[1280]{0:T(1024)(128)(2,1)} %param.17) | copy-start | bytes 7684
  16.1 11.9 %copy-start.7 = (bf16[2,256]{1,0:T(2,128)(2,1)S(1)}, bf16[2,256]{1,0:T(2,128)(2,1)}, u32[]{:S(2)}) copy-start(bf16[2,256]{1,0:T(2,128)(2,1)} %param.19) | copy-start | bytes 3076
  17.2 24.1 %all-to-all-start = ((bf16[2,8,2,64,256]{4,3,2,0,1:T(8,128)(2,1)}), bf16[2,8,2,64,256]{4,3,2,0,1:T(8,128)(2,1)S(1)}, u32[]{:S(2)}, u32[]{:S(2)}) async-start(bf16[2,8,2,64,256]{4,3,2,0,1:T(8,128)(2,1)} %copy.88), calls=%async_computation | async-start | bytes 2097152 | tf_op jit(solution)/shard_map/all_to_all | solution.py:75
  22.4 219.3 %all-gather.8.cloned.1.call-start = ((), (), s32[]{:S(2)}) async-start(), calls=%async_computation.4 | async-start | bytes 14745600 | tf_op jit(solution)/shard_map/all_gather | solution.py:136
  23.2 416.8 %reduce-scatter.2.cloned.1.call-start = ((), (), s32[]{:S(2)}) async-start(), calls=%async_computation.5 | async-start | bytes 13107200 | tf_op jit(solution)/shard_map/reduce_scatter | solution.py:139
  167.8 1.0 copy-start.3
  190.9 20.5 %copy-start.2 = (bf16[1024,2,128]{0,2,1:T(8,128)(2,1)S(1)}, bf16[1024,2,128]{0,2,1:T(8,128)(2,1)}, u32[]{:S(2)}) copy-start(bf16[1024,2,128]{0,2,1:T(8,128)(2,1)} %copy.89) | copy-start | bytes 1572868
  190.9 20.5 %copy-start.4 = (bf16[1024,256]{0,1:T(8,128)(2,1)S(1)}, bf16[1024,256]{0,1:T(8,128)(2,1)}, u32[]{:S(2)}) copy-start(bf16[1024,256]{0,1:T(8,128)(2,1)} %slice.84) | copy-start | bytes 1572868
  261.4 178.6 %copy-start.1 = (s32[8,16]{1,0:T(8,128)S(1)}, s32[8,16]{1,0:T(8,128)}, u32[]{:S(2)}) copy-start(s32[8,16]{1,0:T(8,128)} %param.22) | copy-start | bytes 1540
Sparse Core Ops, SparseCore 0:
  9.2 53.1 all-gather.3
  64.3 74.1 all-gather.5
  140.4 74.0 all-gather.7
  261.6 178.3 reduce-scatter.1
where the time goes:
time: 447 us
  waiting for transfers between devices  263 us (59%)
  matrix products  121 us (27%)
  local copies, waits for them, and re-layouts  24.4 us (5%)
  other arithmetic  18.4 us (4%)
  between operations  14.1 us (3%)
  starting transfers between devices  5.31 us (1%)
    reduce_scatter x1, waiting for transfers between devices, shards(): lax.psum_scatter(partial_out.astype(jnp.bfloat16), 'mp', scatter_dimensio...  179 us
    all_gather x1, waiting for transfers between devices, shards(): lax.all_gather(w_query, 'dp', axis=0, tiled=True)  59.6 us
    sub x2, matrix products, shards(): raised = jnp.exp(logit_scores - top)  42.5 us
    dot_general x2, matrix products, shards(): jnp.einsum('kgqn,nkd->qkgd', weights, all_values, preferred_element_type=...  30.3 us
    dot_general x1, matrix products, shards(): jnp.dot(columns, lax.all_gather(w_query, 'dp', axis=0, tiled=True), prefe...  20 us
    dot_general x1, matrix products, shards(): jnp.dot(attention, lax.all_gather(w_out, 'dp', axis=1, tiled=True), prefe...  19.7 us
    all_gather x1, waiting for transfers between devices, shards(): piece = lax.all_gather(keyvalue_weight, 'dp', axis=0, tiled=True)  18.7 us
  transfers between devices with their start and end apart: 5, of which 4 were waited for; matrix products, arithmetic and copies ran while one was open for 32% of the time, Pallas kernels for 0%

commit v1 on v0

--- a/solution.py
+++ b/solution.py
@@ -8,6 +8,18 @@
 rope_theta = 1000000.0
 norm_eps = 1e-06
 masked_score = -1e30
+
+
+def collect(x, axis, dim):
+    ways, here = (lax.axis_size(axis), lax.axis_index(axis))
+    grown, reach = (x, 1)
+    while reach < ways:
+        theirs = lax.ppermute(grown, axis, [(d, d ^ reach) for d in range(ways)])
+        mine_first = jnp.concatenate([grown, theirs], axis=dim)
+        theirs_first = jnp.concatenate([theirs, grown], axis=dim)
+        grown = jnp.where(here & reach == 0, mine_first, theirs_first)
+        reach = 2 * reach
+    return grown
 
 
 def rms_normed(rows, norm_gain):
@@ -86,11 +98,7 @@
     key_live = jnp.repeat(page_live, page_len)
     normed = rms_normed(tokens, norm_gain)
     columns = normed
-    query = jnp.dot(
-        columns,
-        lax.all_gather(w_query, "dp", axis=0, tiled=True),
-        preferred_element_type=jnp.float32,
-    )
+    query = jnp.dot(columns, collect(w_query, "dp", 0), preferred_element_type=jnp.float32)
     piece = lax.all_gather(keyvalue_weight, "dp", axis=0, tiled=True)
     columns = normed
     keyval = jnp.dot(

time: 447 us -> 654 us (1.46)
  waiting for transfers between devices: 263 us -> 456 us
  other arithmetic: 18.4 us -> 29.4 us
    all_to_all x1, waiting for transfers between devices: 4.06 us -> 182 us  [shards(): lax.all_to_all(outgoing, 'dp', split_axis=1, concat_axis=1, tiled=True)]
    ppermute x0 -> x3, waiting for transfers between devices: none -> 93.6 us  [collect(): theirs = lax.ppermute(grown, axis, [(d, d ^ reach) for d in range(ways)])]
    all_gather x1 -> x0, waiting for transfers between devices: 59.6 us -> none  [shards(): lax.all_gather(w_query, 'dp', axis=0, tiled=True)]
    all_gather x1, waiting for transfers between devices: 18.7 us -> 0.01 us  [shards(): piece = lax.all_gather(keyvalue_weight, 'dp', axis=0, tiled=True)]
    select_n x0 -> x2, other arithmetic: none -> 11.6 us  [collect(): grown = jnp.where(here & reach == 0, mine_first, theirs_first)]
  transfers between devices with their start and end apart: 5 -> 7, of which waited for: 4 -> 4; matrix products, arithmetic and copies ran while one was open for 32% -> 24% of each run, Pallas kernels for 0% -> 0%
where the time goes in v1:
time: 654 us
  waiting for transfers between devices  456 us (70%)
  matrix products  123 us (19%)
  other arithmetic  29.4 us (4%)
  local copies, waits for them, and re-layouts  22.3 us (3%)
  between operations  14.1 us (2%)
  starting transfers between devices  8.91 us (1%)
    all_to_all x1, waiting for transfers between devices, shards(): lax.all_to_all(outgoing, 'dp', split_axis=1, concat_axis=1, tiled=True)  182 us
    reduce_scatter x1, waiting for transfers between devices, shards(): lax.psum_scatter(partial_out.astype(jnp.bfloat16), 'mp', scatter_dimensio...  179 us
    ppermute x3, waiting for transfers between devices, collect(): theirs = lax.ppermute(grown, axis, [(d, d ^ reach) for d in range(ways)])  93.6 us
    sub x2, matrix products, shards(): raised = jnp.exp(logit_scores - top)  41.1 us
    dot_general x2, matrix products, shards(): jnp.einsum('kgqn,nkd->qkgd', weights, all_values, preferred_element_type=...  30.2 us
    dot_general x1, matrix products, shards(): jnp.dot(columns, collect(w_query, 'dp', 0), preferred_element_type=jnp.fl...  23.2 us
    dot_general x1, matrix products, shards(): jnp.dot(attention, lax.all_gather(w_out, 'dp', axis=1, tiled=True), prefe...  19.7 us
  transfers between devices with their start and end apart: 7, of which 4 were waited for; matrix products, arithmetic and copies ran while one was open for 24% of the time, Pallas kernels for 0%

profile of v1, /device:TPU:0, one launch (start us, length us, event | category | flops | bytes accessed | tf_op | source)
XLA Modules:
  0.0 653.6 jit_solution(6211342530754233766)
XLA Ops:
  6.6 0.7 all-gather.3.cloned.1.call-update
  7.3 0.6 collective-permute-start
  7.8 3.5 collective-permute-done
  11.3 3.4 maximum_select_fusion.5
  14.7 2.9 collective-permute-start.1
  17.8 0.6 gather_fusion
  18.5 0.6 gather_fusion.2
  19.1 0.2 reduce_window_sum.11
  19.3 0.6 gather_fusion.3
  19.9 90.1 %collective-permute-done.1 = bf16[1280,1280]{1,0:T(8,128)(2,1)} collective-permute-done((bf16[1280,1280]{1,0:T(8,128)(2,1)S(1)}, bf16[1280,1280]{1,0:T(8,128)(2,1)}, u32[]{:S(2)}, u32[]{:S(2)}) %collective-permute-start.1) | collective-permute-done | bytes 3276832 | tf_op jit(solution)/shard_map/ppermute | solution.py:17
  110.0 8.2 %maximum_select_fusion.2 = bf16[2560,1280]{1,0:T(8,128)(2,1)} fusion(bf16[1280,1280]{1,0:T(8,128)(2,1)} %collective-permute-done.1, bf16[1280,1280]{1,0:T(8,128)(2,1)S(1)} %maximum_select_fusion.5, pred[]{:T(512)S(6)} %eq.66), kind=kLoop, calls=%fused_computation.36 | loop fusion | flops 29491200 | bytes 13107201 | tf_op jit(solution)/shard_map/jit(_where)/select_n | solution.py:20
  118.2 1.8 collective-permute-start.2
  120.0 0.1 select_reduce_fusion
  120.3 2.8 gather_fusion.1
  123.4 0.1 fusion.40
  123.6 0.2 select_select_fusion
  123.8 1.1 copy.88
  124.9 3.6 all-to-all-start
  128.5 0.7 all-gather.5.cloned.1.call-update
  129.3 0.6 dynamic-slice.6
  130.6 0.1 convert_reduce_fusion
  130.7 1.0 multiply_cosine_fusion
  131.7 6.1 fusion.4
  138.2 1.0 copy.91
  139.2 1.0 copy.93
  140.2 0.5 iota_compare_fusion
  140.7 2.7 pad_add_fusion
  143.4 181.5 %all-to-all-done = bf16[2,8,2,64,256]{4,3,2,0,1:T(8,128)(2,1)S(1)} async-done(((bf16[2,8,2,64,256]{4,3,2,0,1:T(8,128)(2,1)}), bf16[2,8,2,64,256]{4,3,2,0,1:T(8,128)(2,1)S(1)}, u32[]{:S(2)}, u32[]{:S(2)}) %all-to-all-start) | async-done | bytes 1048608 | tf_op jit(solution)/shard_map/all_to_all | solution.py:87
  325.0 0.1 squeeze.7
  325.2 0.9 copy.94
  326.0 0.1 squeeze.6
  326.2 1.1 copy.89
  327.3 3.4 copy.106
  330.6 8.9 %fusion.35 = f32[1024,512]{0,1:T(8,128)S(1)} fusion(bf16[5120,512]{1,0:T(8,128)(2,1)S(1)} %bitcast.93, bf16[1024,5120]{1,0:T(8,128)(2,1)} %param.14, f32[5120]{0:T(1024)S(1)} %convert_element_type.65, f32[1024]{0:T(1024)S(1)} %add_rsqrt_fusion, f32[512]{0:T(512)S(1)} %bitcast.101), kind=kOutput, calls=%fused_computation.55 | convolution fusion | flops 5390204928 | bytes 17852416 | tf_op jit(solution)/shard_map/dot_general | solution.py:104
  339.7 0.9 slice.84
  340.6 0.3 copy.104
  340.9 0.3 copy.105
  341.3 2.5 subtract_convert_fusion.1
  343.8 23.2 %fusion.22 = f32[1024,1280]{1,0:T(8,128)} fusion(bf16[2560,1280]{1,0:T(8,128)(2,1)} %collective-permute-done.2, bf16[2560,1280]{1,0:T(8,128)(2,1)} %maximum_select_fusion.2, pred[]{:T(512)S(6)} %eq.65, bf16[1024,5120]{1,0:T(8,128)(2,1)} %param.14, f32[5120]{0:T(1024)S(1)} %convert_element_type.65, f32[1024]{0:T(1024)S(1)} %add_rsqrt_fusion, ...), kind=kOutput, calls=%fused_computation.37 | convolution fusion | flops 13503037440 | bytes 28865536 | tf_op jit(solution)/shard_map/dot_general | solution.py:101
  367.0 5.9 copy.95
  372.9 3.5 subtract_convert_fusion
  376.4 0.3 fusion.38
  376.7 20.6 %fusion.59 = (f32[2,5,512]{2,1,0:T(8,128)S(1)}, f32[2,5,512,2048]{2,3,1,0:T(8,128)}) fusion(pred[512,2048]{0,1:T(8,128)(4,1)} %get-tuple-element.45, bf16[512,2,5,128]{0,3,2,1:T(8,128)(2,1)S(1)} %bitcast.98, bf16[1024,2,64]{2,0,1:T(8,128)(2,1)} %get-tuple-element.36, bf16[1024,2,64]{2,0,1:T(8,128)(2,1)} %get-tuple-element.35, ...), kind=kOutput, calls=%fused_computation.113 | convolution fusion | flops 2729445376 | bytes 45371392 | tf_op jit(solution)/shard_map/sub | solution.py:135
  397.3 20.4 %fusion.58 = (f32[2,5,512]{2,1,0:T(8,128)S(1)}, f32[2,5,512,2048]{2,3,1,0:T(8,128)}) fusion(pred[512,2048]{0,1:T(8,128)(4,1)} %get-tuple-element.46, bf16[512,2,5,128]{0,3,2,1:T(8,128)(2,1)S(1)} %bitcast.97, bf16[1024,2,64]{2,0,1:T(8,128)(2,1)} %get-tuple-element.36, bf16[1024,2,64]{2,0,1:T(8,128)(2,1)} %get-tuple-element.35, ...), kind=kOutput, calls=%fused_computation.112 | convolution fusion | flops 2729445376 | bytes 45371392 | tf_op jit(solution)/shard_map/sub | solution.py:135
  417.8 14.6 %fusion.34 = bf16[2,128,5,512]{3,1,2,0:T(8,128)(2,1)S(1)} fusion(f32[2,5,512,2048]{2,3,1,0:T(8,128)} %get-tuple-element.51, f32[2,5,512]{2,1,0:T(8,128)S(1)} %get-tuple-element.50, bf16[1024,2,128]{0,2,1:T(8,128)(2,1)S(1)} %bitcast.99, bf16[1024,2,128]{0,2,1:T(8,128)(2,1)S(1)} %copy-done.3), kind=kOutput, calls=%fused_computation.54 | convolution fusion | flops 2708078592 | bytes 44322816 | tf_op jit(solution)/shard_map/kgqn,nkd->qkgd/dot_general | solution.py:137
  432.3 15.6 %fusion.33 = bf16[2,128,5,512]{3,1,2,0:T(8,128)(2,1)} fusion(f32[2,5,512,2048]{2,3,1,0:T(8,128)} %get-tuple-element.49, f32[2,5,512]{2,1,0:T(8,128)S(1)} %get-tuple-element.48, bf16[1024,2,128]{0,2,1:T(8,128)(2,1)S(1)} %bitcast.100, bf16[1024,2,128]{0,2,1:T(8,128)(2,1)S(1)} %copy-done.3), kind=kOutput, calls=%fused_computation.53 | convolution fusion | flops 2708078592 | bytes 44322816 | tf_op jit(solution)/shard_map/kgqn,nkd->qkgd/dot_general | solution.py:137
  447.9 19.7 %convolution_convert_fusion = bf16[1024,5120]{1,0:T(8,128)(2,1)} fusion(bf16[1280,5120]{1,0:T(8,128)(2,1)} %all-gather.5.cloned.1.call-done, bf16[512,1280]{0,1:T(8,128)(2,1)} %bitcast.103, bf16[512,1280]{0,1:T(8,128)(2,1)S(1)} %bitcast.102), kind=kOutput, calls=%fused_computation.35 | convolution fusion | flops 13432258560 | bytes 26214400 | tf_op jit(solution)/shard_map/dot_general | solution.py:142
  467.7 179.4 %reduce-scatter.2.cloned.1.call-done = bf16[1024,1280]{1,0:T(8,128)(2,1)} async-done(((bf16[1024,5120]{1,0:T(8,128)(2,1)}), bf16[1024,1280]{1,0:T(8,128)(2,1)}) %reduce-scatter.2.cloned.1.call-update) | async-done | bytes 2621456 | tf_op jit(solution)/shard_map/reduce_scatter | solution.py:147
  (63 shorter events, 1.6 us)
Async XLA Ops:
  6.5 11.9 %copy-start = (s32[8,16]{1,0:T(8,128)S(1)}, s32[8,16]{1,0:T(8,128)}, u32[]{:S(2)}) copy-start(s32[8,16]{1,0:T(8,128)} %param.22) | copy-start | bytes 1540
  6.5 11.1 %copy-start.10 = (s32[8]{0:T(128)S(1)}, s32[8]{0:T(128)}, u32[]{:S(2)}) copy-start(s32[8]{0:T(128)} %param.25) | copy-start | bytes 100
  6.5 11.2 %copy-start.2 = (s32[8]{0:T(128)S(1)}, s32[8]{0:T(128)}, u32[]{:S(2)}) copy-start(s32[8]{0:T(128)} %param.24) | copy-start | bytes 100
  6.5 12.7 %copy-start.6 = (s32[8,16]{1,0:T(8,128)S(1)}, s32[8,16]{1,0:T(8,128)}, u32[]{:S(2)}) copy-start(s32[8,16]{1,0:T(8,128)} %param.23) | copy-start | bytes 1540
  6.5 320.7 %all-gather.3.cloned.1.call-start = ((), (), s32[]{:S(2)}) async-start(), calls=%async_computation.2 | async-start | bytes 5898240 | tf_op jit(solution)/shard_map/all_gather | solution.py:102
  7.3 4.0 collective-permute-start
  14.7 95.3 %collective-permute-start.1 = (bf16[1280,1280]{1,0:T(8,128)(2,1)S(1)}, bf16[1280,1280]{1,0:T(8,128)(2,1)}, u32[]{:S(2)}, u32[]{:S(2)}) collective-permute-start(bf16[1280,1280]{1,0:T(8,128)(2,1)S(1)} %maximum_select_fusion.5), channel_id=1, source_target_pairs={{0,8},{4,12},{8,0},{12,4},{16,24},{20,28},{24,16},{28,20},{1,9},{5... | collective-permute-start | bytes 9830408 | tf_op jit(solution)/shard_map/ppermute | solution.py:17
  118.2 225.6 %collective-permute-start.2 = (bf16[2560,1280]{1,0:T(8,128)(2,1)}, bf16[2560,1280]{1,0:T(8,128)(2,1)}, u32[]{:S(2)}, u32[]{:S(2)}) collective-permute-start(bf16[2560,1280]{1,0:T(8,128)(2,1)} %maximum_select_fusion.2), channel_id=1, source_target_pairs={{0,16},{4,20},{8,24},{12,28},{16,0},{20,4},{24,8},{28,12},{1,17},{... | collective-permute-start | bytes 19660808 | tf_op jit(solution)/shard_map/ppermute | solution.py:17
  123.1 7.6 %copy-start.9 = (bf16[2,256]{1,0:T(2,128)(2,1)S(1)}, bf16[2,256]{1,0:T(2,128)(2,1)}, u32[]{:S(2)}) copy-start(bf16[2,256]{1,0:T(2,128)(2,1)} %param.19) | copy-start | bytes 3076
  124.9 200.0 %all-to-all-start = ((bf16[2,8,2,64,256]{4,3,2,0,1:T(8,128)(2,1)}), bf16[2,8,2,64,256]{4,3,2,0,1:T(8,128)(2,1)S(1)}, u32[]{:S(2)}, u32[]{:S(2)}) async-start(bf16[2,8,2,64,256]{4,3,2,0,1:T(8,128)(2,1)} %copy.88), calls=%async_computation | async-start | bytes 2097152 | tf_op jit(solution)/shard_map/all_to_all | solution.py:87
  128.5 319.4 %all-gather.5.cloned.1.call-start = ((), (), s32[]{:S(2)}) async-start(), calls=%async_computation.3 | async-start | bytes 14745600 | tf_op jit(solution)/shard_map/all_gather | solution.py:144
  129.2 517.9 %reduce-scatter.2.cloned.1.call-start = ((), (), s32[]{:S(2)}) async-start(), calls=%async_computation.4 | async-start | bytes 13107200 | tf_op jit(solution)/shard_map/reduce_scatter | solution.py:147
  131.7 6.2 copy-start.7
  131.7 6.2 copy-start.8
  372.9 3.8 copy-start.4
  397.3 20.4 %copy-start.3 = (bf16[1024,2,128]{0,2,1:T(8,128)(2,1)S(1)}, bf16[1024,2,128]{0,2,1:T(8,128)(2,1)}, u32[]{:S(2)}) copy-start(bf16[1024,2,128]{0,2,1:T(8,128)(2,1)} %copy.89) | copy-start | bytes 1572868
  397.3 20.4 %copy-start.5 = (bf16[1024,256]{0,1:T(8,128)(2,1)S(1)}, bf16[1024,256]{0,1:T(8,128)(2,1)}, u32[]{:S(2)}) copy-start(bf16[1024,256]{0,1:T(8,128)(2,1)} %slice.84) | copy-start | bytes 1572868
  467.7 179.4 %copy-start.1 = (s32[8,16]{1,0:T(8,128)S(1)}, s32[8,16]{1,0:T(8,128)}, u32[]{:S(2)}) copy-start(s32[8,16]{1,0:T(8,128)} %param.22) | copy-start | bytes 1540
Sparse Core Ops, SparseCore 0:
  9.2 64.4 all-gather.2
  131.2 128.5 all-gather.4
  467.8 179.2 reduce-scatter.1
